TPU v7x, 256 devices: a whole 4x4x8 slice. The times are simulated.
256 devices in a mesh: row: 32 (over x, y, core), col: 8 (over z).
Axes of the slice: x: 4, y: 4, z: 8, core: 2. Of those that a mesh axis runs over, the one named last changes fastest.
Arguments:
- a_matrix: float32 [2048, 2048], P('row', 'col'), may hold values from -0.9 to 0.9
- b_matrix: float32 [2048, 2048], P('row', 'col'), may hold values from -0.9 to 0.9
- a_panel: float32 [2048, 1024], P('row', 'col'), may hold values from -0.9 to 0.9
- b_panel: float32 [2048, 1024], P('row', 'col'), may hold values from -0.9 to 0.9
Outputs:
- triangle: float32 [1024, 1024], P('row', 'col')
- pencil_cross: float32 [2048, 2048], P('row', 'col')
All inputs are finite; a program needn't handle non-finite values.
Results may differ from a plain program's by a relative error of at most 0.0003.
Values sent between devices are 32-bit elements; how exact they have to be, the bound alone decides.
A program may use at most 64 MiB of HBM per device.

v0:
```python
import jax
import jax.numpy as jnp
from jax import lax
from jax.sharding import PartitionSpec as P

HIGHEST = lax.Precision.HIGHEST


def in_one_piece(arrays, axis, dim, along):
    widths = [a.shape[along] for a in arrays]
    both = jnp.concatenate(arrays, axis=along)
    whole = lax.all_gather(both, axis, axis=dim, tiled=True)
    return tuple(jnp.split(whole, [sum(widths[:k]) for k in range(1, len(widths))], axis=along))


def in_blocks(x, dim, count):
    lengths = x.shape
    blocks = x.reshape(*lengths[:dim], count, lengths[dim] // count, *lengths[dim + 1 :])
    return jnp.moveaxis(blocks, dim, 0)


def summed_on_arrival(x, axis, dim):
    blocks = in_blocks(x, dim, lax.axis_size(axis))
    arrived = lax.all_to_all(blocks, axis, split_axis=0, concat_axis=0, tiled=True)
    return arrived.sum(axis=0)


def from_everyone(x, axis):
    count = lax.axis_size(axis)
    return lax.all_to_all(jnp.broadcast_to(x[None], (count, *x.shape)), axis, 0, 0, tiled=True)


def joined_along(blocks, dim):
    blocks = jnp.moveaxis(blocks, 0, dim)
    lengths = blocks.shape
    return blocks.reshape(*lengths[:dim], lengths[dim] * lengths[dim + 1], *lengths[dim + 2 :])


def gather_directly(x, axis, dim):
    blocks = from_everyone(x, axis)
    return joined_along(blocks, dim)


def local(a_matrix, b_matrix, a_panel, b_panel):
    row_count = a_matrix.shape[0]
    panel_width = a_panel.shape[1]
    full_a, full_pa, full_pb = (
        lax.all_gather(a_matrix, "col", axis=1, tiled=True),
        *in_one_piece((a_panel, b_panel), "col", 1, 0),
    )
    stacked = jnp.concatenate([full_pb, -full_pa], 0)
    own_block = jnp.concatenate([b_panel, -a_panel], 0)
    partial_gram = jnp.dot(own_block.T, stacked, precision=HIGHEST)
    gram_part = summed_on_arrival(partial_gram, "row", 1)
    gram_rows = gather_directly(gram_part, "row", 1)
    gram_matrix = lax.all_gather(gram_rows, "col", axis=0, tiled=True)
    lower_factor = jnp.linalg.cholesky(gram_matrix)
    q_rows = jax.scipy.linalg.solve_triangular(lower_factor, stacked.T, lower=True).T
    upper_rows = q_rows[:row_count]
    lower_rows = q_rows[row_count:]
    row_index = lax.axis_index("row")
    col_index = lax.axis_index("col")
    tri_rows = gram_matrix.shape[0] // lax.axis_size("row")
    corner = lax.dynamic_slice(
        lower_factor, (col_index * panel_width, row_index * tri_rows), (panel_width, tri_rows)
    )
    triangle = corner.T
    partial_z = jnp.dot(lower_rows.T, b_matrix, precision=HIGHEST)
    z_part = summed_on_arrival(partial_z, "row", 0)
    z_columns = gather_directly(z_part, "row", 0)
    v_block = jnp.dot(upper_rows, z_columns, precision=HIGHEST)
    pencil_cross = summed_on_arrival(-jnp.dot(full_a.T, v_block, precision=HIGHEST), "row", 0)
    return (triangle, pencil_cross)


def solution(mesh):
    in_specs = (P("row", "col"), P("row", "col"), P("row", "col"), P("row", "col"))
    out_specs = (P("row", "col"), P("row", "col"))
    return jax.shard_map(local, mesh=mesh, in_specs=in_specs, out_specs=out_specs, check_vma=False)
```

profile of v0, /device:TPU:1, one launch (start us, length us, event | category | flops | bytes accessed | tf_op | source)
XLA Modules:
  0.0 574.5 jit_solution(9497342517812801916)
XLA Ops:
  8.8 23.7 %all_gather.9 = f32[128,1024]{1,0:T(8,128)S(1)} all-gather(f32[128,128]{1,0:T(8,128)S(1)} %pad_maximum_fusion.2), channel_id=1, replica_groups=mesh['row'=32,'col'=8] {'col'}, dimensions={1}, use_global_device_ids=true | all-gather | bytes 589824 | tf_op jit(solution)/shard_map/all_gather | solution.py:12
  34.3 25.4 %all_to_all.25 = f32[32,128,32]{1,2,0:T(8,128)S(1)} all-to-all(f32[32,128,32]{1,2,0:T(8,128)S(1)} %bitcast.125), channel_id=1, replica_groups=mesh['row'=32,'col'=8] {'row'}, dimensions={0} | all-to-all | bytes 1048576 | tf_op jit(solution)/shard_map/all_to_all | solution.py:24
  59.8 15.1 %all_to_all.26 = f32[32,128,32]{1,2,0:T(8,128)} all-to-all(f32[32,128,32]{1,2,0:T(8,128)S(1)} %broadcast_in_dim.6), channel_id=1, replica_groups=mesh['row'=32,'col'=8] {'row'}, dimensions={0} | all-to-all | bytes 1048576 | tf_op jit(solution)/shard_map/all_to_all | solution.py:30
  75.0 53.9 %all-gather.2.cloned.1.call-done = f32[1024,1024]{0,1:T(8,128)} async-done(((f32[128,1024]{0,1:T(8,128)}), f32[1024,1024]{0,1:T(8,128)}) %all-gather.2.cloned.1.call-update) | async-done | bytes 4194320 | tf_op jit(solution)/shard_map/all_gather | solution.py:56
  128.9 5.8 %copy.16 = f32[1024,1024]{1,0:T(8,128)} copy(f32[1024,1024]{0,1:T(8,128)} %all-gather.2.cloned.1.call-done) | data formatting | bytes 8388608 | tf_op jit(solution)/shard_map/all_gather | solution.py:56
  134.7 4.4 fusion
  141.0 11.7 %cholesky.223 = f32[128,128]{1,0:T(8,128)S(1)} custom-call(f32[128,128]{1,0:T(8,128)S(1)} %cholesky.580), custom_call_target="Cholesky" | custom-call | tf_op jit(solution)/shard_map/jit(cholesky)/cholesky | solution.py:57
  152.8 2.5 cholesky.255
  155.3 9.8 %custom-call.63 = f32[1,128,128]{1,2,0:T(8,128)S(1)} custom-call(f32[1,128,128]{2,1,0:T(8,128)S(1)} %get-tuple-element.74), custom_call_target="InvertDiagBlocksLowerTriangular" | custom-call | tf_op jit(solution)/shard_map/jit(cholesky)/cholesky | solution.py:57
  168.9 11.9 %cholesky.244 = f32[128,128]{1,0:T(8,128)S(1)} custom-call(f32[128,128]{1,0:T(8,128)S(1)} %cholesky.584), custom_call_target="Cholesky" | custom-call | tf_op jit(solution)/shard_map/jit(cholesky)/cholesky | solution.py:57
  182.3 9.8 %custom-call.64 = f32[1,128,128]{1,2,0:T(8,128)S(1)} custom-call(f32[1,128,128]{2,1,0:T(8,128)S(1)} %get-tuple-element.71), custom_call_target="InvertDiagBlocksLowerTriangular" | custom-call | tf_op jit(solution)/shard_map/jit(cholesky)/cholesky | solution.py:57
  195.4 11.7 %cholesky.468 = f32[128,128]{1,0:T(8,128)S(1)} custom-call(f32[128,128]{1,0:T(8,128)S(1)} %cholesky.589), custom_call_target="Cholesky" | custom-call | tf_op jit(solution)/shard_map/jit(cholesky)/cholesky | solution.py:57
  208.4 9.8 %custom-call.65 = f32[1,128,128]{1,2,0:T(8,128)S(1)} custom-call(f32[1,128,128]{2,1,0:T(8,128)S(1)} %get-tuple-element.68), custom_call_target="InvertDiagBlocksLowerTriangular" | custom-call | tf_op jit(solution)/shard_map/jit(cholesky)/cholesky | solution.py:57
  219.4 2.3 convolution_subtract_fusion.2
  221.8 11.9 %cholesky.487 = f32[128,128]{1,0:T(8,128)S(1)} custom-call(f32[128,128]{1,0:T(8,128)S(1)} %cholesky.594), custom_call_target="Cholesky" | custom-call | tf_op jit(solution)/shard_map/jit(cholesky)/cholesky | solution.py:57
  235.0 9.8 %custom-call.66 = f32[1,128,128]{1,2,0:T(8,128)S(1)} custom-call(f32[1,128,128]{2,1,0:T(8,128)S(1)} %get-tuple-element.65), custom_call_target="InvertDiagBlocksLowerTriangular" | custom-call | tf_op jit(solution)/shard_map/jit(cholesky)/cholesky | solution.py:57
  245.9 2.3 convolution_subtract_fusion.3
  248.3 11.7 %cholesky.506 = f32[128,128]{1,0:T(8,128)S(1)} custom-call(f32[128,128]{1,0:T(8,128)S(1)} %cholesky.599), custom_call_target="Cholesky" | custom-call | tf_op jit(solution)/shard_map/jit(cholesky)/cholesky | solution.py:57
  261.4 10.2 %custom-call.67 = f32[1,128,128]{1,2,0:T(8,128)S(1)} custom-call(f32[1,128,128]{2,1,0:T(8,128)S(1)} %get-tuple-element.62), custom_call_target="InvertDiagBlocksLowerTriangular" | custom-call | tf_op jit(solution)/shard_map/jit(cholesky)/cholesky | solution.py:57
  274.9 11.7 %cholesky.526 = f32[128,128]{1,0:T(8,128)S(1)} custom-call(f32[128,128]{1,0:T(8,128)S(1)} %cholesky.604), custom_call_target="Cholesky" | custom-call | tf_op jit(solution)/shard_map/jit(cholesky)/cholesky | solution.py:57
  287.9 9.8 %custom-call.68 = f32[1,128,128]{1,2,0:T(8,128)S(1)} custom-call(f32[1,128,128]{2,1,0:T(8,128)S(1)} %get-tuple-element.59), custom_call_target="InvertDiagBlocksLowerTriangular" | custom-call | tf_op jit(solution)/shard_map/jit(cholesky)/cholesky | solution.py:57
  300.7 11.8 %cholesky.546 = f32[128,128]{1,0:T(8,128)S(1)} custom-call(f32[128,128]{1,0:T(8,128)S(1)} %cholesky.609), custom_call_target="Cholesky" | custom-call | tf_op jit(solution)/shard_map/jit(cholesky)/cholesky | solution.py:57
  313.8 9.8 %custom-call.69 = f32[1,128,128]{1,2,0:T(8,128)S(1)} custom-call(f32[1,128,128]{2,1,0:T(8,128)S(1)} %get-tuple-element.56), custom_call_target="InvertDiagBlocksLowerTriangular" | custom-call | tf_op jit(solution)/shard_map/jit(cholesky)/cholesky | solution.py:57
  326.2 11.7 %cholesky.564 = f32[128,128]{1,0:T(8,128)S(1)} custom-call(f32[128,128]{1,0:T(8,128)S(1)} %convolution_subtract_fusion.11), custom_call_target="Cholesky" | custom-call | tf_op jit(solution)/shard_map/jit(cholesky)/cholesky | solution.py:57
  344.9 6.6 %fusion.1 = (f32[1024,1024]{1,0:T(8,128)}, f32[1024,1024]{1,0:T(8,128)}) fusion(f32[1024,1024]{1,0:T(8,128)} %get-tuple-element.54, pred[]{:T(512)S(6)} %cholesky.579), kind=kLoop, calls=%fused_computation.6 | loop fusion | flops 4194304 | bytes 12582913 | tf_op jit(solution)/shard_map/jit(_solve_triangular)/triangular_solve | solution.py:58
  351.6 23.2 %while.1 = (s32[]{:T(128)}, f32[1024,1024]{1,0:T(8,128)}, s32[8,2]{0,1:T(2,128)S(1)}, f32[8,128,128]{2,1,0:T(8,128)S(1)}, s32[]{:T(128)}) while((s32[]{:T(128)}, f32[1024,1024]{1,0:T(8,128)}, s32[8,2]{0,1:T(2,128)S(1)}, f32[8,128,128]{2,1,0:T(8,128)S(1)}, s32[]{:T(128)}) %tuple.64), condition=%wide.while_cond, body=%wide.while_body.sunk | while | flops 2 | bytes 131181 | solution.py:58
  374.8 78.8 %custom-call.70 = f32[8,128,128]{1,2,0:T(8,128)S(1)} custom-call(f32[8,128,128]{2,1,0:T(8,128)S(1)} %get-tuple-element.9), custom_call_target="InvertDiagBlocksLowerTriangular" | custom-call | tf_op jit(solution)/shard_map/jit(_solve_triangular)/triangular_solve | solution.py:58
  467.8 27.9 %all_to_all.27 = f32[32,32,256]{2,1,0:T(8,128)S(1)} all-to-all(f32[32,32,256]{2,1,0:T(8,128)S(1)} %bitcast.121), channel_id=1, replica_groups=mesh['row'=32,'col'=8] {'row'}, dimensions={0} | all-to-all | bytes 2097152 | tf_op jit(solution)/shard_map/all_to_all | solution.py:24
  496.9 3.9 all-to-all-start.3
  500.9 20.7 %all_gather.11 = f32[64,2048]{1,0:T(8,128)S(1)} all-gather(f32[64,256]{1,0:T(8,128)S(1)} %copy-done.2), channel_id=1, replica_groups=mesh['row'=32,'col'=8] {'col'}, dimensions={1}, use_global_device_ids=true | all-gather | bytes 589824 | tf_op jit(solution)/shard_map/all_gather | solution.py:48
  526.4 12.0 %all-to-all-start.4 = ((f32[32,64,256]{2,1,0:T(8,128)}), f32[32,64,256]{2,1,0:T(8,128)S(1)}, u32[]{:S(2)}, u32[]{:S(2)}) async-start(f32[32,64,256]{2,1,0:T(8,128)} %bitcast.119), calls=%async_computation.4 | async-start | bytes 4194304 | tf_op jit(solution)/shard_map/all_to_all | solution.py:24
  540.0 26.7 %all-to-all-done.4 = f32[32,64,256]{2,1,0:T(8,128)S(1)} async-done(((f32[32,64,256]{2,1,0:T(8,128)}), f32[32,64,256]{2,1,0:T(8,128)S(1)}, u32[]{:S(2)}, u32[]{:S(2)}) %all-to-all-start.4) | async-done | bytes 2097184 | tf_op jit(solution)/shard_map/all_to_all | solution.py:24
  (103 shorter events, 79.3 us)
Async XLA Ops:
  7.2 459.6 %copy-start = (f32[64,256]{1,0:T(8,128)S(1)}, f32[64,256]{1,0:T(8,128)}, u32[]{:S(2)}) copy-start(f32[64,256]{1,0:T(8,128)} %param.5) | copy-start | bytes 196612
  7.2 121.7 %all-gather.2.cloned.1.call-start = ((), (), s32[]{:S(2)}) async-start(), calls=%async_computation.5 | async-start | bytes 4718592 | tf_op jit(solution)/shard_map/all_gather | solution.py:56
  139.1 1.9 copy-start.1
  466.5 34.4 %copy-start.2 = (f32[64,256]{1,0:T(8,128)S(1)}, f32[64,256]{1,0:T(8,128)}, u32[]{:S(2)}) copy-start(f32[64,256]{1,0:T(8,128)} %param.4) | copy-start | bytes 196612
  496.9 24.7 %all-to-all-start.3 = ((f32[32,32,256]{2,1,0:T(8,128)}), f32[32,32,256]{2,1,0:T(8,128)S(1)}, u32[]{:S(2)}, u32[]{:S(2)}) async-start(f32[32,32,256]{2,1,0:T(8,128)} %broadcast_in_dim.7), calls=%async_computation.3 | async-start | bytes 2097152 | tf_op jit(solution)/shard_map/all_to_all | solution.py:30
  526.4 40.3 %all-to-all-start.4 = ((f32[32,64,256]{2,1,0:T(8,128)}), f32[32,64,256]{2,1,0:T(8,128)S(1)}, u32[]{:S(2)}, u32[]{:S(2)}) async-start(f32[32,64,256]{2,1,0:T(8,128)} %bitcast.119), calls=%async_computation.4 | async-start | bytes 4194304 | tf_op jit(solution)/shard_map/all_to_all | solution.py:24
Sparse Core Ops, SparseCore 0:
  75.0 53.8 all-gather.1
where the time goes:
time: 579 us; the launch traced here: 575 us
  other arithmetic  265 us (46%)
  blocking collectives  113 us (20%)
  waiting for transfers between devices  80.6 us (14%)
  matrix products  41.5 us (7%)
  local copies, waits for them, and re-layouts  39 us (7%)
  between operations  19.7 us (3%)
  starting transfers between devices  15.9 us (3%)
    another operation x30, other arithmetic, local(): lower_factor = jnp.linalg.cholesky(gram_matrix)  172 us
    another operation x3, other arithmetic, local(): jax.scipy.linalg.solve_triangular(lower_factor, stacked.T, lower=True)  85.4 us
    all_gather x1, waiting for transfers between devices, local(): gram_matrix = lax.all_gather(gram_rows, 'col', axis=0, tiled=True)  53.9 us
    all_to_all x2, blocking collectives, summed_on_arrival(): lax.all_to_all(blocks, axis, split_axis=0, concat_axis=0, tiled=True)  53.3 us
    all_to_all x1, waiting for transfers between devices, summed_on_arrival(): lax.all_to_all(blocks, axis, split_axis=0, concat_axis=0, tiled=True)  26.7 us
    all_gather x1, blocking collectives, in_one_piece(): whole = lax.all_gather(both, axis, axis=dim, tiled=True)  23.7 us
    another operation x24, local copies, waits for them, and re-layouts  23 us
    another operation x14, matrix products, local(): lower_factor = jnp.linalg.cholesky(gram_matrix)  22.7 us
  transfers between devices with their start and end apart: 3, of which 2 were waited for; matrix products, arithmetic and copies ran while one was open for 0% of the time, Pallas kernels for 0%

commit v1 on v0

--- a/solution.py
+++ b/solution.py
@@ -1,9 +1,20 @@
+import functools
 import jax
 import jax.numpy as jnp
 from jax import lax
 from jax.sharding import PartitionSpec as P
 
 HIGHEST = lax.Precision.HIGHEST
+
+
+def _report_roads(u, lane_axis):
+    spare = tuple((u for _ in range(lax.axis_size(lane_axis))))
+    step_out = jnp.stack(spare, 0)
+    v_next = lax.all_to_all(step_out, axis_name=lane_axis, concat_axis=0, split_axis=0)
+    return jnp.concatenate(v_next, axis=0)
+
+
+pass_inputs = functools.partial(_report_roads, lane_axis="col")
 
 
 def in_one_piece(arrays, axis, dim, along):
@@ -53,7 +64,7 @@
     partial_gram = jnp.dot(own_block.T, stacked, precision=HIGHEST)
     gram_part = summed_on_arrival(partial_gram, "row", 1)
     gram_rows = gather_directly(gram_part, "row", 1)
-    gram_matrix = lax.all_gather(gram_rows, "col", axis=0, tiled=True)
+    gram_matrix = pass_inputs(gram_rows)
     lower_factor = jnp.linalg.cholesky(gram_matrix)
     q_rows = jax.scipy.linalg.solve_triangular(lower_factor, stacked.T, lower=True).T
     upper_rows = q_rows[:row_count]

time: 579 us -> 612 us (1.057)
  waiting for transfers between devices: 80.6 us -> 123 us
  between operations: 19.7 us -> 6.34 us
  local copies, waits for them, and re-layouts: 39 us -> 47.7 us
  blocking collectives: 113 us -> 105 us
    all_to_all x0 -> x1, waiting for transfers between devices: none -> 96.6 us  [_report_roads(): lax.all_to_all(step_out, axis_name=lane_axis, concat_axis=0, split_axis=0)]
    all_gather x1 -> x0, waiting for transfers between devices: 53.9 us -> none  [local(): gram_matrix = lax.all_gather(gram_rows, 'col', axis=0, tiled=True)]
    reshape x0 -> x2, local copies, waits for them, and re-layouts: none -> 10.5 us  [_report_roads(): return jnp.concatenate(v_next, axis=0)]
    all_to_all x2, blocking collectives: 53.3 us -> 45.8 us  [summed_on_arrival(): lax.all_to_all(blocks, axis, split_axis=0, concat_axis=0, tiled=True)]
    another operation x24 -> x25, local copies, waits for them, and re-layouts: 23 us -> 25.3 us
where the time goes in v1:
time: 612 us; the launch traced here: 607 us
  other arithmetic  264 us (43%)
  waiting for transfers between devices  123 us (20%)
  blocking collectives  105 us (17%)
  local copies, waits for them, and re-layouts  47.7 us (8%)
  matrix products  39.6 us (6%)
  starting transfers between devices  20.9 us (3%)
  between operations  6.34 us (1%)
    another operation x30, other arithmetic, local(): lower_factor = jnp.linalg.cholesky(gram_matrix)  172 us
    all_to_all x1, waiting for transfers between devices, _report_roads(): lax.all_to_all(step_out, axis_name=lane_axis, concat_axis=0, split_axis=0)  96.6 us
    another operation x3, other arithmetic, local(): jax.scipy.linalg.solve_triangular(lower_factor, stacked.T, lower=True)  85.4 us
    all_to_all x2, blocking collectives, summed_on_arrival(): lax.all_to_all(blocks, axis, split_axis=0, concat_axis=0, tiled=True)  45.8 us
    all_to_all x1, waiting for transfers between devices, summed_on_arrival(): lax.all_to_all(blocks, axis, split_axis=0, concat_axis=0, tiled=True)  26.7 us
    all_gather x1, blocking collectives, in_one_piece(): whole = lax.all_gather(both, axis, axis=dim, tiled=True)  23.7 us
    another operation x24, local copies, waits for them, and re-layouts  23 us
    another operation x14, matrix products, local(): lower_factor = jnp.linalg.cholesky(gram_matrix)  22.7 us
  transfers between devices with their start and end apart: 3, of which 2 were waited for; matrix products, arithmetic and copies ran while one was open for 0% of the time, Pallas kernels for 0%

profile of v1, /device:TPU:1, one launch (start us, length us, event | category | flops | bytes accessed | tf_op | source)
XLA Modules:
  0.0 607.0 jit_solution(16648122044439986812)
XLA Ops:
  3.2 23.7 %all_gather.6 = f32[128,1024]{0,1:T(8,128)S(1)} all-gather(f32[128,128]{0,1:T(8,128)S(1)} %pad_maximum_fusion.2), channel_id=1, replica_groups=mesh['row'=32,'col'=8] {'col'}, dimensions={1}, use_global_device_ids=true | all-gather | bytes 589824 | tf_op jit(solution)/shard_map/all_gather | solution.py:23
  28.6 25.4 %all_to_all.30 = f32[32,128,32]{1,2,0:T(8,128)S(1)} all-to-all(f32[32,128,32]{1,2,0:T(8,128)S(1)} %bitcast.133), channel_id=1, replica_groups=mesh['row'=32,'col'=8] {'row'}, dimensions={0} | all-to-all | bytes 1048576 | tf_op jit(solution)/shard_map/all_to_all | solution.py:35
  54.0 15.0 %all_to_all.31 = f32[32,128,32]{1,2,0:T(8,128)S(1)} all-to-all(f32[32,128,32]{1,2,0:T(8,128)S(1)} %broadcast_in_dim.6), channel_id=1, replica_groups=mesh['row'=32,'col'=8] {'row'}, dimensions={0} | all-to-all | bytes 1048576 | tf_op jit(solution)/shard_map/all_to_all | solution.py:41
  71.3 4.5 all-to-all-start.2
  76.1 96.6 %all-to-all-done.2 = f32[8,128,1024]{1,2,0:T(8,128)} async-done(((f32[8,128,1024]{1,2,0:T(8,128)}), f32[8,128,1024]{1,2,0:T(8,128)}, u32[]{:S(2)}, u32[]{:S(2)}) %all-to-all-start.2) | async-done | bytes 4194336 | tf_op jit(solution)/shard_map/all_to_all | solution.py:13
  172.7 4.7 copy_bitcast_fusion
  177.5 5.8 copy.30
  183.2 4.1 fusion
  189.3 11.7 %cholesky.223 = f32[128,128]{1,0:T(8,128)S(1)} custom-call(f32[128,128]{1,0:T(8,128)S(1)} %cholesky.580), custom_call_target="Cholesky" | custom-call | tf_op jit(solution)/shard_map/jit(cholesky)/cholesky | solution.py:68
  201.0 2.5 cholesky.255
  203.5 9.8 %custom-call.63 = f32[1,128,128]{1,2,0:T(8,128)S(1)} custom-call(f32[1,128,128]{2,1,0:T(8,128)S(1)} %get-tuple-element.76), custom_call_target="InvertDiagBlocksLowerTriangular" | custom-call | tf_op jit(solution)/shard_map/jit(cholesky)/cholesky | solution.py:68
  217.1 11.9 %cholesky.244 = f32[128,128]{1,0:T(8,128)S(1)} custom-call(f32[128,128]{1,0:T(8,128)S(1)} %cholesky.584), custom_call_target="Cholesky" | custom-call | tf_op jit(solution)/shard_map/jit(cholesky)/cholesky | solution.py:68
  230.5 9.8 %custom-call.64 = f32[1,128,128]{1,2,0:T(8,128)S(1)} custom-call(f32[1,128,128]{2,1,0:T(8,128)S(1)} %get-tuple-element.73), custom_call_target="InvertDiagBlocksLowerTriangular" | custom-call | tf_op jit(solution)/shard_map/jit(cholesky)/cholesky | solution.py:68
  243.6 11.7 %cholesky.468 = f32[128,128]{1,0:T(8,128)S(1)} custom-call(f32[128,128]{1,0:T(8,128)S(1)} %cholesky.589), custom_call_target="Cholesky" | custom-call | tf_op jit(solution)/shard_map/jit(cholesky)/cholesky | solution.py:68
  256.6 9.8 %custom-call.65 = f32[1,128,128]{1,2,0:T(8,128)S(1)} custom-call(f32[1,128,128]{2,1,0:T(8,128)S(1)} %get-tuple-element.70), custom_call_target="InvertDiagBlocksLowerTriangular" | custom-call | tf_op jit(solution)/shard_map/jit(cholesky)/cholesky | solution.py:68
  270.0 11.9 %cholesky.487 = f32[128,128]{1,0:T(8,128)S(1)} custom-call(f32[128,128]{1,0:T(8,128)S(1)} %cholesky.594), custom_call_target="Cholesky" | custom-call | tf_op jit(solution)/shard_map/jit(cholesky)/cholesky | solution.py:68
  283.2 9.8 %custom-call.66 = f32[1,128,128]{1,2,0:T(8,128)S(1)} custom-call(f32[1,128,128]{2,1,0:T(8,128)S(1)} %get-tuple-element.67), custom_call_target="InvertDiagBlocksLowerTriangular" | custom-call | tf_op jit(solution)/shard_map/jit(cholesky)/cholesky | solution.py:68
  296.5 11.7 %cholesky.506 = f32[128,128]{1,0:T(8,128)S(1)} custom-call(f32[128,128]{1,0:T(8,128)S(1)} %cholesky.599), custom_call_target="Cholesky" | custom-call | tf_op jit(solution)/shard_map/jit(cholesky)/cholesky | solution.py:68
  309.6 10.2 %custom-call.67 = f32[1,128,128]{1,2,0:T(8,128)S(1)} custom-call(f32[1,128,128]{2,1,0:T(8,128)S(1)} %get-tuple-element.64), custom_call_target="InvertDiagBlocksLowerTriangular" | custom-call | tf_op jit(solution)/shard_map/jit(cholesky)/cholesky | solution.py:68
  323.1 11.7 %cholesky.526 = f32[128,128]{1,0:T(8,128)S(1)} custom-call(f32[128,128]{1,0:T(8,128)S(1)} %cholesky.604), custom_call_target="Cholesky" | custom-call | tf_op jit(solution)/shard_map/jit(cholesky)/cholesky | solution.py:68
  336.1 9.8 %custom-call.68 = f32[1,128,128]{1,2,0:T(8,128)S(1)} custom-call(f32[1,128,128]{2,1,0:T(8,128)S(1)} %get-tuple-element.61), custom_call_target="InvertDiagBlocksLowerTriangular" | custom-call | tf_op jit(solution)/shard_map/jit(cholesky)/cholesky | solution.py:68
  348.9 11.8 %cholesky.546 = f32[128,128]{1,0:T(8,128)S(1)} custom-call(f32[128,128]{1,0:T(8,128)S(1)} %cholesky.609), custom_call_target="Cholesky" | custom-call | tf_op jit(solution)/shard_map/jit(cholesky)/cholesky | solution.py:68
  362.0 9.8 %custom-call.69 = f32[1,128,128]{1,2,0:T(8,128)S(1)} custom-call(f32[1,128,128]{2,1,0:T(8,128)S(1)} %get-tuple-element.58), custom_call_target="InvertDiagBlocksLowerTriangular" | custom-call | tf_op jit(solution)/shard_map/jit(cholesky)/cholesky | solution.py:68
  374.4 11.7 %cholesky.564 = f32[128,128]{1,0:T(8,128)S(1)} custom-call(f32[128,128]{1,0:T(8,128)S(1)} %convolution_subtract_fusion.11), custom_call_target="Cholesky" | custom-call | tf_op jit(solution)/shard_map/jit(cholesky)/cholesky | solution.py:68
  393.1 6.6 %fusion.1 = (f32[1024,1024]{1,0:T(8,128)}, f32[1024,1024]{1,0:T(8,128)}) fusion(f32[1024,1024]{1,0:T(8,128)} %get-tuple-element.56, pred[]{:T(512)S(6)} %cholesky.579), kind=kLoop, calls=%fused_computation.7 | loop fusion | flops 4194304 | bytes 12582913 | tf_op jit(solution)/shard_map/jit(_solve_triangular)/triangular_solve | solution.py:69
  399.8 23.2 %while.1 = (s32[]{:T(128)}, f32[1024,1024]{1,0:T(8,128)}, s32[8,2]{0,1:T(2,128)S(1)}, f32[8,128,128]{2,1,0:T(8,128)S(1)}, s32[]{:T(128)}) while((s32[]{:T(128)}, f32[1024,1024]{1,0:T(8,128)}, s32[8,2]{0,1:T(2,128)S(1)}, f32[8,128,128]{2,1,0:T(8,128)S(1)}, s32[]{:T(128)}) %tuple.65), condition=%wide.while_cond, body=%wide.while_body.sunk | while | flops 2 | bytes 131181 | solution.py:69
  423.0 78.8 %custom-call.70 = f32[8,128,128]{1,2,0:T(8,128)S(1)} custom-call(f32[8,128,128]{2,1,0:T(8,128)S(1)} %get-tuple-element.9), custom_call_target="InvertDiagBlocksLowerTriangular" | custom-call | tf_op jit(solution)/shard_map/jit(_solve_triangular)/triangular_solve | solution.py:69
  514.5 20.5 %all_to_all.32 = f32[32,32,256]{2,1,0:T(8,128)S(1)} all-to-all(f32[32,32,256]{2,1,0:T(8,128)S(1)} %bitcast.130), channel_id=1, replica_groups=mesh['row'=32,'col'=8] {'row'}, dimensions={0} | all-to-all | bytes 2097152 | tf_op jit(solution)/shard_map/all_to_all | solution.py:35
  536.2 3.9 all-to-all-start.4
  540.1 20.4 %all_gather.7 = f32[64,2048]{1,0:T(8,128)S(1)} all-gather(f32[64,256]{1,0:T(8,128)S(1)} %copy-done.2), channel_id=1, replica_groups=mesh['row'=32,'col'=8] {'col'}, dimensions={1}, use_global_device_ids=true | all-gather | bytes 589824 | tf_op jit(solution)/shard_map/all_gather | solution.py:59
  565.3 12.4 %all-to-all-start.5 = ((f32[32,64,256]{2,1,0:T(8,128)}), f32[32,64,256]{2,1,0:T(8,128)S(1)}, u32[]{:S(2)}, u32[]{:S(2)}) async-start(f32[32,64,256]{2,1,0:T(8,128)} %bitcast.128), calls=%async_computation.5 | async-start | bytes 4194304 | tf_op jit(solution)/shard_map/all_to_all | solution.py:35
  579.3 26.7 %all-to-all-done.5 = f32[32,64,256]{2,1,0:T(8,128)S(1)} async-done(((f32[32,64,256]{2,1,0:T(8,128)}), f32[32,64,256]{2,1,0:T(8,128)S(1)}, u32[]{:S(2)}, u32[]{:S(2)}) %all-to-all-start.5) | async-done | bytes 2097184 | tf_op jit(solution)/shard_map/all_to_all | solution.py:35
  (106 shorter events, 85.6 us)
Async XLA Ops:
  0.6 512.9 %copy-start = (f32[64,256]{1,0:T(8,128)S(1)}, f32[64,256]{1,0:T(8,128)}, u32[]{:S(2)}) copy-start(f32[64,256]{1,0:T(8,128)} %param.5) | copy-start | bytes 196612
  71.3 101.4 %all-to-all-start.2 = ((f32[8,128,1024]{1,2,0:T(8,128)}), f32[8,128,1024]{1,2,0:T(8,128)}, u32[]{:S(2)}, u32[]{:S(2)}) async-start(f32[8,128,1024]{1,2,0:T(8,128)} %stack.3), calls=%async_computation.2 | async-start | bytes 8388608 | tf_op jit(solution)/shard_map/all_to_all | solution.py:13
  187.3 1.9 copy-start.1
  513.2 26.9 %copy-start.2 = (f32[64,256]{1,0:T(8,128)S(1)}, f32[64,256]{1,0:T(8,128)}, u32[]{:S(2)}) copy-start(f32[64,256]{1,0:T(8,128)} %param.4) | copy-start | bytes 196612
  536.2 24.4 %all-to-all-start.4 = ((f32[32,32,256]{2,1,0:T(8,128)}), f32[32,32,256]{2,1,0:T(8,128)S(1)}, u32[]{:S(2)}, u32[]{:S(2)}) async-start(f32[32,32,256]{2,1,0:T(8,128)} %broadcast_in_dim.7), calls=%async_computation.4 | async-start | bytes 2097152 | tf_op jit(solution)/shard_map/all_to_all | solution.py:41
  565.3 40.8 %all-to-all-start.5 = ((f32[32,64,256]{2,1,0:T(8,128)}), f32[32,64,256]{2,1,0:T(8,128)S(1)}, u32[]{:S(2)}, u32[]{:S(2)}) async-start(f32[32,64,256]{2,1,0:T(8,128)} %bitcast.128), calls=%async_computation.5 | async-start | bytes 4194304 | tf_op jit(solution)/shard_map/all_to_all | solution.py:35
